TPU v7x, 256 devices: a whole 4x4x8 slice. The times are simulated.
256 devices in a mesh: gx: 32 (over y, z), gy: 8 (over x, core).
Axes of the slice: x: 4, y: 4, z: 8, core: 2. Of those that a mesh axis runs over, the one named last changes fastest.
Arguments:
- right_sides: bfloat16 [64, 32, 8, 256], P('gx', 'gy'), may hold values from -6 to 6
- leaf_order: int32 [64, 32, 256], P('gx', 'gy'), may hold values from 0 to 255, each once within a row
- leaf_basis: bfloat16 [64, 32, 64, 256], P('gx', 'gy'), may hold values from -0.375 to 0.375
- near_blocks: bfloat16 [64, 32, 256, 2304], P('gx', 'gy'), may hold values from -0.125 to 0.125
- leaf_coupling: bfloat16 [64, 32, 64, 1728], P('gx', 'gy'), may hold values from -0.15625 to 0.15625
- leaf_transfer: bfloat16 [64, 32, 64, 64], P('gx', 'gy'), may hold values from -0.5 to 0.5
- box_coupling: bfloat16 [32, 16, 64, 1728], P('gx', 'gy'), may hold values from -0.15625 to 0.15625
- box_transfer: bfloat16 [32, 16, 64, 64], P('gx', 'gy'), may hold values from -0.5 to 0.5
- coarse_coupling: bfloat16 [32, 8, 64, 4096], P('gx', 'gy'), may hold values from -0.0625 to 0.0625
Outputs:
- product: float32 [64, 32, 8, 256], P('gx', 'gy')
Inputs may be any that keep to these rules, and one draw needn't show every extreme that they name: In every leaf, leaf_order names each of 0 to 255 once.
All inputs are finite; a program needn't handle non-finite values.
Results may differ from a plain program's by a relative error of at most 0.0003.
Values may be sent and summed in bfloat16 or wider, within the bound.
A program may use at most 128 MiB of HBM per device.

v0:
```python
import jax
import jax.numpy as jnp
import numpy as np
from jax import lax
from jax.sharding import Mesh
from jax.sharding import PartitionSpec as P

GX = ("gx_0", "gx_1")
GY = ("gy_0", "gy_1")


exact_mode = lax.Precision.HIGHEST


def with_halo(block, sides, width):
    for axis, dim in sides:
        count = lax.axis_size(axis)
        forward = [(i, i + 1) for i in range(count - 1)]
        backward = [(target, source) for source, target in forward]
        low = lax.ppermute(
            lax.slice_in_dim(block, block.shape[dim] - width, None, axis=dim), axis, forward
        )
        high = lax.ppermute(lax.slice_in_dim(block, 0, width, axis=dim), axis, backward)
        block = jnp.concatenate([low, block, high], axis=dim)
    return block


def copy_for_each(value, axis):
    length = lax.axis_size(axis)
    return lax.all_to_all(
        jnp.broadcast_to(value[None], (length, *value.shape)), axis, 0, 0, tiled=True
    )


def joined_along(tiles, dim):
    dims = list(tiles.shape[1:])
    dims[dim] *= tiles.shape[0]
    return jnp.moveaxis(tiles, 0, dim).reshape(dims)


def gather_axes(value, axes, dim):
    far, near = axes
    leading = copy_for_each(value, far)
    tiles = jnp.swapaxes(copy_for_each(leading, near), 0, 1)
    return joined_along(tiles.reshape(-1, *value.shape), dim)


def side_by_side(arrays, axis, dim, along):
    widths = [a.shape[along] for a in arrays]
    both = jnp.concatenate(arrays, axis=along)
    whole = gather_axes(both, axis, dim)
    return tuple(jnp.split(whole, [sum(widths[:k]) for k in range(1, len(widths))], axis=along))


def swapped(value, axis, stride):
    return lax.ppermute(value, axis, [(i, i ^ 1 << stride) for i in range(lax.axis_size(axis))])


def slot_table():
    chosen_all = np.zeros((2, 2, 27), np.int32)
    for u in range(2):
        for v in range(2):
            chosen = [
                a * 6 + b
                for a in range(6)
                for b in range(6)
                if max(abs(a - 2 - u), abs(b - 2 - v)) > 1
            ]
            chosen_all[u, v] = np.array(chosen, np.int32)
    return chosen_all


def pick_list(flat, listed):
    return jnp.stack([flat[int(place)] for place in listed], 0)


def body(
    right_sides,
    leaf_order,
    leaf_basis,
    near_blocks,
    leaf_coupling,
    leaf_transfer,
    box_coupling,
    box_transfer,
    coarse_coupling,
):
    n_rhs = right_sides.shape[2]
    n_points = right_sides.shape[3]
    rank_size = leaf_basis.shape[2]
    coeff_width = n_rhs * rank_size
    gx_size = lax.axis_size(GX)
    gy_size = lax.axis_size(GY)
    row_index = lax.axis_index(GX)
    col_index = lax.axis_index(GY)
    parity = row_index % 2
    table = slot_table()
    positions = jnp.arange(n_points, dtype=jnp.int32)
    selector = leaf_order[:, :, :, None] == positions[None, None, None, :]
    ordered = jnp.einsum(
        "ucsp,uckp->ucsk",
        right_sides,
        selector.astype(jnp.bfloat16),
        preferred_element_type=jnp.float32,
    ).astype(jnp.bfloat16)
    padded_points = with_halo(ordered, ((GX, 0), (GY, 1)), 1)
    leaf_coeffs = jnp.einsum(
        "ucsp,uckp->ucsk", ordered, leaf_basis, preferred_element_type=jnp.float32
    )
    padded_coeffs = with_halo(leaf_coeffs.reshape(2, 4, coeff_width), ((GX, 0), (GY, 1)), 2)
    leaf_up = leaf_transfer.reshape(2, 2, 2, rank_size, rank_size)
    box_coeffs = jnp.einsum(
        "uwvsk,uwvkm->wsm",
        leaf_coeffs.reshape(2, 2, 2, n_rhs, rank_size),
        leaf_up,
        precision=exact_mode,
        preferred_element_type=jnp.float32,
    )
    box_up = box_transfer.reshape(2, rank_size, rank_size)
    pair_part = jnp.einsum(
        "vsk,vkm->sm", box_coeffs, box_up, precision=exact_mode, preferred_element_type=jnp.float32
    )
    member_coeffs = box_coeffs.reshape(1, 2, coeff_width)
    member_part = pair_part.reshape(1, 1, coeff_width)
    every_coeffs, every_parts = side_by_side(
        (member_coeffs, member_part), (("gx_0", "gx_1"), ("gy_0", "gy_1")), 0, 1
    )
    all_boxes = every_coeffs.reshape(gx_size, -1, coeff_width)
    all_parts = every_parts.reshape(gx_size, -1, coeff_width)
    padded_boxes = jnp.pad(all_boxes, ((2, 2), (2, 2), (0, 0)))
    box_window = lax.dynamic_slice(
        padded_boxes, (2 * (row_index // 2), 2 * col_index, 0), (6, 6, coeff_width)
    )
    coarse_flat = (all_parts[0::2] + all_parts[1::2]).reshape(-1, coeff_width)
    stacked_points = [
        padded_points[1 + a : 3 + a, 1 + b : 5 + b] for a in (-1, 0, 1) for b in (-1, 0, 1)
    ]
    neighbours = jnp.stack(stacked_points, 2)
    blocks = near_blocks.reshape(2, 4, n_points, 9, n_points)
    near_values = jnp.einsum(
        "ucqsp,ucaqp->ucsa", neighbours, blocks, preferred_element_type=jnp.float32
    )
    windows = jnp.stack([padded_coeffs[:, 2 * w : 2 * w + 6] for w in range(2)], 0).reshape(
        2, 36, coeff_width
    )
    leaf_sources = jnp.stack(
        [
            jnp.stack(
                [jnp.stack([windows[:, int(place)] for place in table[u, v]], 1) for v in range(2)],
                1,
            )
            for u in range(2)
        ],
        1,
    )
    leaf_sources = leaf_sources.reshape(2, 2, 2, 27, n_rhs, rank_size)
    leaf_couplings = leaf_coupling.reshape(2, 2, 2, rank_size, 27, rank_size)
    leaf_far = jnp.einsum(
        "wuvtsj,uwvktj->uwvsk",
        leaf_sources,
        leaf_couplings,
        precision=exact_mode,
        preferred_element_type=jnp.float32,
    )
    window_flat = box_window.reshape(36, coeff_width)
    even_sources = jnp.stack([pick_list(window_flat, table[0, v]) for v in range(2)], 0)
    odd_sources = jnp.stack([pick_list(window_flat, table[1, v]) for v in range(2)], 0)
    box_sources = jnp.where(parity == 0, even_sources, odd_sources).reshape(2, 27, n_rhs, rank_size)
    box_couplings = box_coupling.reshape(2, rank_size, 27, rank_size)
    box_far = jnp.einsum(
        "vtsj,vktj->vsk",
        box_sources,
        box_couplings,
        precision=exact_mode,
        preferred_element_type=jnp.float32,
    )
    half_count = coarse_flat.shape[0] // 2
    my_sources = lax.dynamic_slice_in_dim(coarse_flat, parity * half_count, half_count, 0)
    source = parity * half_count + jnp.arange(half_count, dtype=jnp.int32)
    far_mask = (jnp.abs(source // gy_size - row_index // 2) > 1) | (
        jnp.abs(source % gy_size - col_index) > 1
    )
    masked = (my_sources * far_mask[:, None].astype(jnp.float32)).reshape(
        half_count, n_rhs, rank_size
    )
    coarse_couplings = coarse_coupling.reshape(rank_size, half_count, rank_size)
    half_far = jnp.einsum(
        "tsj,ktj->sk",
        masked,
        coarse_couplings,
        precision=exact_mode,
        preferred_element_type=jnp.float32,
    )
    coarse_far = half_far + swapped(half_far, GX, 0)
    box_down = (
        jnp.einsum(
            "sm,vkm->vsk",
            coarse_far,
            box_up,
            precision=exact_mode,
            preferred_element_type=jnp.float32,
        )
        + box_far
    )
    leaf_down = (
        jnp.einsum(
            "wsm,uwvkm->uwvsk",
            box_down,
            leaf_up,
            precision=exact_mode,
            preferred_element_type=jnp.float32,
        )
        + leaf_far
    )
    leaf_down = leaf_down.reshape(2, 4, n_rhs, rank_size)
    values = (
        jnp.einsum(
            "ucsk,uckp->ucsp",
            leaf_down,
            leaf_basis,
            precision=exact_mode,
            preferred_element_type=jnp.float32,
        )
        + near_values
    )
    return jnp.einsum(
        "ucsk,uckp->ucsp",
        values,
        selector.astype(jnp.float32),
        precision=exact_mode,
        preferred_element_type=jnp.float32,
    )


def solution(mesh):
    finer = Mesh(mesh.devices.reshape(4, 8, 4, 2), ("gx_0", "gx_1", "gy_0", "gy_1"))
    placed = (
        P(GX, GY, None, None),
        P(GX, GY, None),
        P(GX, GY, None, None),
        P(GX, GY, None, None),
        P(GX, GY, None, None),
        P(GX, GY, None, None),
        P(GX, GY, None, None),
        P(GX, GY, None, None),
        P(GX, GY, None, None),
    )
    return jax.shard_map(
        body, mesh=finer, in_specs=placed, out_specs=P(GX, GY, None, None), check_vma=False
    )
```

profile of v0, /device:TPU:8, one launch (start us, length us, event | category | flops | bytes accessed | tf_op | source)
XLA Modules:
  0.0 111.0 jit_solution(16248420187369500237)
XLA Ops:
  0.0 1.4 %fusion.6 = bf16[2,4,256,8]{2,3,1,0:T(8,128)(2,1)S(1)} fusion(bf16[2,4,8,256]{3,2,1,0:T(8,128)(2,1)} %param.9, s32[2,4,256]{2,1,0:T(4,128)} %param.10), kind=kOutput, calls=%fused_computation.10 | convolution fusion | flops 8929280 | bytes 73728 | tf_op jit(solution)/shard_map/ucsp,uckp->ucsk/dot_general | solution.py:100
  1.4 0.2 fusion.55
  1.6 0.1 reshape.133
  1.7 7.7 %collective-permute-start.2 = (f32[2,4,512]{2,1,0:T(4,128)S(1)}, f32[2,4,512]{2,1,0:T(4,128)S(1)}, u32[]{:S(2)}, u32[]{:S(2)}) collective-permute-start(f32[2,4,512]{2,1,0:T(4,128)S(1)} %reshape.133), channel_id=1, source_target_pairs={{8,0},{16,8},{24,16},{32,24},{40,32},{48,40},{56,48},{64,56},{72,6... | collective-permute-start | bytes 49160 | tf_op jit(solution)/shard_map/ppermute | solution.py:23
  9.3 1.9 %collective-permute-start.1 = (f32[2,4,512]{2,1,0:T(4,128)S(1)}, f32[2,4,512]{2,1,0:T(4,128)S(1)}, u32[]{:S(2)}, u32[]{:S(2)}) collective-permute-start(f32[2,4,512]{2,1,0:T(4,128)S(1)} %reshape.133), channel_id=1, source_target_pairs={{0,8},{8,16},{16,24},{24,32},{32,40},{40,48},{48,56},{56,64},{64,7... | collective-permute-start | bytes 49160 | tf_op jit(solution)/shard_map/ppermute | solution.py:20
  11.3 1.9 %collective-permute-start.5 = (bf16[1,4,8,256]{3,2,1,0:T(8,128)(2,1)S(1)}, bf16[1,4,8,256]{3,2,1,0:T(8,128)(2,1)S(1)}, u32[]{:S(2)}, u32[]{:S(2)}) collective-permute-start(bf16[1,4,8,256]{3,2,1,0:T(8,128)(2,1)S(1)} %get-tuple-element.41), channel_id=1, source_target_pairs={{0,8},{8,16},{16,24},{24,32},{32,40},{40,48},{48,56},{56,64},{64,7... | collective-permute-start | bytes 49160 | tf_op jit(solution)/shard_map/ppermute | solution.py:20
  13.2 6.0 %collective-permute-start.6 = (bf16[1,4,8,256]{3,2,1,0:T(8,128)(2,1)S(1)}, bf16[1,4,8,256]{3,2,1,0:T(8,128)(2,1)S(1)}, u32[]{:S(2)}, u32[]{:S(2)}) collective-permute-start(bf16[1,4,8,256]{3,2,1,0:T(8,128)(2,1)S(1)} %get-tuple-element.42), channel_id=1, source_target_pairs={{8,0},{16,8},{24,16},{32,24},{40,32},{48,40},{56,48},{64,56},{72,6... | collective-permute-start | bytes 49160 | tf_op jit(solution)/shard_map/ppermute | solution.py:23
  19.2 1.1 %convolution_bitcast_fusion.3 = f32[2,8,64]{2,1,0:T(8,128)S(1)} fusion(f32[2,2,2,8,64]{4,3,2,1,0:T(8,128)S(1)} %bitcast.121, bf16[2,2,2,64,64]{4,3,2,1,0:T(8,128)(2,1)} %bitcast.119), kind=kOutput, calls=%fused_computation.18 | convolution fusion | flops 3145728 | bytes 86016 | tf_op jit(solution)/shard_map/uwvsk,uwvkm->wsm/dot_general | solution.py:112
  20.4 0.1 reshape.123
  20.4 0.9 convolution_bitcast_fusion.5
  21.4 0.1 reshape.125
  21.5 0.8 broadcast_in_dim.9
  22.3 7.1 %all-to-all-start = ((f32[32,1,3,512]{3,1,2,0:T(1,128)}), f32[32,1,3,512]{3,1,2,0:T(1,128)S(1)}, u32[]{:S(2)}, u32[]{:S(2)}) async-start(f32[32,1,3,512]{3,1,2,0:T(1,128)} %broadcast_in_dim.9), calls=%async_computation | async-start | bytes 393216 | tf_op jit(solution)/shard_map/all_to_all | solution.py:30
  29.5 2.7 %reshape.132 = bf16[2,64,27,64]{3,2,1,0:T(8,128)(2,1)} reshape(bf16[1,2,64,1728]{3,2,1,0:T(8,128)(2,1)} %param.15) | data formatting | bytes 884736 | tf_op jit(solution)/shard_map/reshape | solution.py:169
  32.2 2.1 %reshape.129 = bf16[64,64,64]{2,1,0:T(8,128)(2,1)S(1)} reshape(bf16[1,1,64,4096]{3,2,1,0:T(8,128)(2,1)} %param.17) | data formatting | bytes 1048576 | tf_op jit(solution)/shard_map/reshape | solution.py:186
  34.2 5.0 %reshape.134 = bf16[2,2,2,64,27,64]{5,4,3,2,1,0:T(8,128)(2,1)} reshape(bf16[2,4,64,1728]{3,2,1,0:T(8,128)(2,1)S(1)} %copy-done.2) | data formatting | bytes 3538944 | tf_op jit(solution)/shard_map/reshape | solution.py:157
  39.2 12.6 %copy.109 = bf16[2,4,256,2304]{2,3,1,0:T(8,128)(2,1)} copy(bf16[2,4,256,2304]{3,2,1,0:T(8,128)(2,1)} %param.12) | data formatting | bytes 18874368 | tf_op args[3]
  51.9 0.0 collective-permute-done.1
  51.9 0.0 collective-permute-done.5
  51.9 0.0 collective-permute-done.6
  51.9 1.3 %collective-permute-start.8 = (bf16[4,1,8,256]{3,2,1,0:T(8,128)(2,1)S(1)}, bf16[4,1,8,256]{3,2,1,0:T(8,128)(2,1)S(1)}, u32[]{:S(2)}, u32[]{:S(2)}) collective-permute-start(bf16[4,1,8,256]{3,2,1,0:T(8,128)(2,1)S(1)} %get-tuple-element.35), channel_id=1, source_target_pairs={{1,0},{2,1},{3,2},{4,3},{5,4},{6,5},{7,6},{9,8},{10,9},{11,10},{12... | collective-permute-start | bytes 49160 | tf_op jit(solution)/shard_map/ppermute | solution.py:23
  53.2 3.0 %collective-permute-start.7 = (bf16[4,1,8,256]{3,2,1,0:T(8,128)(2,1)S(1)}, bf16[4,1,8,256]{3,2,1,0:T(8,128)(2,1)S(1)}, u32[]{:S(2)}, u32[]{:S(2)}) collective-permute-start(bf16[4,1,8,256]{3,2,1,0:T(8,128)(2,1)S(1)} %get-tuple-element.36), channel_id=1, source_target_pairs={{0,1},{1,2},{2,3},{3,4},{4,5},{5,6},{6,7},{8,9},{9,10},{10,11},{11... | collective-permute-start | bytes 49160 | tf_op jit(solution)/shard_map/ppermute | solution.py:20
  56.3 0.0 collective-permute-done.2
  56.3 1.3 %collective-permute-start.4 = (f32[6,2,512]{2,1,0:T(2,128)S(1)}, f32[6,2,512]{2,1,0:T(2,128)S(1)}, u32[]{:S(2)}, u32[]{:S(2)}) collective-permute-start(f32[6,2,512]{2,1,0:T(2,128)S(1)} %get-tuple-element.39), channel_id=1, source_target_pairs={{1,0},{2,1},{3,2},{4,3},{5,4},{6,5},{7,6},{9,8},{10,9},{11,10},{12... | collective-permute-start | bytes 73736 | tf_op jit(solution)/shard_map/ppermute | solution.py:23
  57.6 3.6 %collective-permute-start.3 = (f32[6,2,512]{2,1,0:T(2,128)S(1)}, f32[6,2,512]{2,1,0:T(2,128)S(1)}, u32[]{:S(2)}, u32[]{:S(2)}) collective-permute-start(f32[6,2,512]{2,1,0:T(2,128)S(1)} %get-tuple-element.40), channel_id=1, source_target_pairs={{0,1},{1,2},{2,3},{3,4},{4,5},{5,6},{6,7},{8,9},{9,10},{10,11},{11... | collective-permute-start | bytes 73736 | tf_op jit(solution)/shard_map/ppermute | solution.py:20
  61.3 0.0 collective-permute-done.8
  61.3 0.0 collective-permute-done.7
  61.4 5.6 %fusion = f32[2,4,8,256,1]{3,2,0,1,4:T(8,128)} fusion(bf16[2,4,256,9,256]{2,4,3,1,0:T(8,128)(2,1)} %bitcast.110, bf16[2,4,9,8,256]{4,3,1,0,2:T(8,128)(2,1)S(1)} %fusion.26), kind=kOutput, calls=%fused_computation | convolution fusion | flops 75497472 | bytes 9797632 | tf_op jit(solution)/shard_map/ucqsp,ucaqp->ucsa/dot_general | solution.py:140
  67.1 0.0 collective-permute-done.4
  67.1 0.0 collective-permute-done.3
  67.2 0.0 all-to-all-done
  67.3 1.4 %broadcast_in_dim.22 = f32[8,32,1,3,512]{4,1,3,2,0:T(8,128)} broadcast(f32[32,3,512]{2,0,1:T(8,128)S(1)} %bitcast.118), dimensions={1,3,4} | broadcast | bytes 1769472 | tf_op jit(solution)/shard_map/broadcast_in_dim | solution.py:31
  68.6 5.3 %all-to-all-start.1 = ((f32[8,32,1,3,512]{4,1,3,2,0:T(8,128)}), f32[8,32,1,3,512]{4,1,3,2,0:T(8,128)S(1)}, u32[]{:S(2)}, u32[]{:S(2)}) async-start(f32[8,32,1,3,512]{4,1,3,2,0:T(8,128)} %broadcast_in_dim.22), calls=%async_computation.1 | async-start | bytes 3145728 | tf_op jit(solution)/shard_map/all_to_all | solution.py:30
  74.1 0.1 pad_maximum_fusion
  74.2 0.8 reshape.145
  74.9 0.1 reshape.147
  75.0 0.8 reshape.148
  75.8 0.1 reshape.146
  75.9 6.8 %fusion.8 = f32[2,2,2,8,64]{4,3,2,0,1:T(8,128)} fusion(bf16[2,2,2,64,27,64]{5,4,3,2,1,0:T(8,128)(2,1)} %reshape.134, f32[2,1,1,27,8,64]{5,4,3,0,2,1:T(8,128)} %reshape.148, f32[2,1,1,27,8,64]{5,4,3,0,2,1:T(8,128)S(1)} %reshape.147, f32[2,1,1,27,8,64]{5,4,3,0,2,1:T(8,128)S(1)} %reshape.146, f32[2,1,1,27,8,64]{5,4,3,0,2,1:T(8,128)} %reshape.145), kind=kOutput, calls=%fused_computation.13 | convolution fusion | flops 85266432 | bytes 2228224 | tf_op jit(solution)/shard_map/wuvtsj,uwvktj->uwvsk/dot_general | solution.py:158
  82.7 12.9 %all-to-all-done.1 = f32[8,32,1,3,512]{4,1,3,2,0:T(8,128)S(1)} async-done(((f32[8,32,1,3,512]{4,1,3,2,0:T(8,128)}), f32[8,32,1,3,512]{4,1,3,2,0:T(8,128)S(1)}, u32[]{:S(2)}, u32[]{:S(2)}) %all-to-all-start.1) | async-done | bytes 1572896 | tf_op jit(solution)/shard_map/all_to_all | solution.py:30
  95.6 0.9 copy.154
  96.5 0.8 slice_bitcast_fusion
  97.3 0.1 split.9
  97.4 0.8 copy.95
  98.2 0.7 reshape.130
  98.9 0.0 copy-start.3
  98.9 0.7 pad_dynamic-slice_fusion
  99.6 0.9 reshape.131
  100.6 1.1 add_bitcast_fusion
  101.8 0.1 stack.118
  101.8 0.1 stack.113
  101.9 0.1 stack.115
  102.0 0.1 stack.120
  102.1 0.1 dynamic-slice_multiply_fusion
  102.2 0.1 reshape.128
  102.3 1.3 %convolution_bitcast_fusion.4 = f32[8,64]{1,0:T(8,128)S(1)} fusion(f32[64,8,64]{2,1,0:T(8,128)S(1)} %reshape.128, bf16[64,64,64]{2,1,0:T(8,128)(2,1)S(1)} %reshape.129), kind=kOutput, calls=%fused_computation.19 | convolution fusion | flops 25165824 | bytes 657408 | tf_op jit(solution)/shard_map/tsj,ktj->sk/dot_general | solution.py:187
  103.6 1.5 %collective-permute-start = (f32[8,64]{1,0:T(8,128)S(1)}, f32[8,64]{1,0:T(8,128)S(1)}, u32[]{:S(2)}, u32[]{:S(2)}) collective-permute-start(f32[8,64]{1,0:T(8,128)S(1)} %convolution_bitcast_fusion.4), channel_id=1, source_target_pairs={{0,8},{8,0},{16,24},{24,16},{32,40},{40,32},{48,56},{56,48},{64,72... | collective-permute-start | bytes 6152 | tf_op jit(solution)/shard_map/ppermute | solution.py:56
  105.0 1.0 convolution_bitcast_fusion.1
  106.1 1.1 collective-permute-done
  107.2 0.9 fusion.12
  108.1 1.2 %fusion.7 = f32[2,2,2,8,64]{4,3,2,0,1:T(8,128)S(1)} fusion(f32[2,2,2,8,64]{4,3,2,0,1:T(8,128)} %fusion.8, f32[2,8,64,1,1]{2,1,4,3,0:T(8,128)S(1)} %fusion.12, bf16[2,2,2,64,64]{4,3,2,1,0:T(8,128)(2,1)S(1)} %bitcast.120), kind=kOutput, calls=%fused_computation.12 | convolution fusion | flops 3149824 | bytes 102400 | tf_op jit(solution)/shard_map/wsm,uwvkm->uwvsk/dot_general | solution.py:206
  109.3 0.0 copy-done.4
  109.4 0.2 convolution_add_fusion
  109.6 1.4 %fusion.4 = f32[2,4,8,256]{3,2,1,0:T(8,128)} fusion(f32[2,4,8,256]{3,2,1,0:T(8,128)S(1)} %convolution_add_fusion, s32[2,4,256]{2,1,0:T(4,128)S(1)} %copy-done.5), kind=kOutput, calls=%fused_computation.5 | convolution fusion | flops 50855936 | bytes 139264 | tf_op jit(solution)/shard_map/ucsk,uckp->ucsp/dot_general | solution.py:226
  (46 shorter events, 0.5 us)
Async XLA Ops:
  0.0 1.4 %copy-start = (bf16[2,4,64,256]{3,2,1,0:T(8,128)(2,1)S(1)}, bf16[2,4,64,256]{3,2,1,0:T(8,128)(2,1)}, u32[]{:S(2)}) copy-start(bf16[2,4,64,256]{3,2,1,0:T(8,128)(2,1)} %param.11) | copy-start | bytes 786436
  0.0 34.2 %copy-start.2 = (bf16[2,4,64,1728]{3,2,1,0:T(8,128)(2,1)S(1)}, bf16[2,4,64,1728]{3,2,1,0:T(8,128)(2,1)}, u32[]{:S(2)}) copy-start(bf16[2,4,64,1728]{3,2,1,0:T(8,128)(2,1)} %param.13) | copy-start | bytes 5308420
  1.7 54.6 %collective-permute-start.2 = (f32[2,4,512]{2,1,0:T(4,128)S(1)}, f32[2,4,512]{2,1,0:T(4,128)S(1)}, u32[]{:S(2)}, u32[]{:S(2)}) collective-permute-start(f32[2,4,512]{2,1,0:T(4,128)S(1)} %reshape.133), channel_id=1, source_target_pairs={{8,0},{16,8},{24,16},{32,24},{40,32},{48,40},{56,48},{64,56},{72,6... | collective-permute-start | bytes 49160 | tf_op jit(solution)/shard_map/ppermute | solution.py:23
  9.3 42.6 %collective-permute-start.1 = (f32[2,4,512]{2,1,0:T(4,128)S(1)}, f32[2,4,512]{2,1,0:T(4,128)S(1)}, u32[]{:S(2)}, u32[]{:S(2)}) collective-permute-start(f32[2,4,512]{2,1,0:T(4,128)S(1)} %reshape.133), channel_id=1, source_target_pairs={{0,8},{8,16},{16,24},{24,32},{32,40},{40,48},{48,56},{56,64},{64,7... | collective-permute-start | bytes 49160 | tf_op jit(solution)/shard_map/ppermute | solution.py:20
  11.3 40.6 %collective-permute-start.5 = (bf16[1,4,8,256]{3,2,1,0:T(8,128)(2,1)S(1)}, bf16[1,4,8,256]{3,2,1,0:T(8,128)(2,1)S(1)}, u32[]{:S(2)}, u32[]{:S(2)}) collective-permute-start(bf16[1,4,8,256]{3,2,1,0:T(8,128)(2,1)S(1)} %get-tuple-element.41), channel_id=1, source_target_pairs={{0,8},{8,16},{16,24},{24,32},{32,40},{40,48},{48,56},{56,64},{64,7... | collective-permute-start | bytes 49160 | tf_op jit(solution)/shard_map/ppermute | solution.py:20
  13.2 38.7 %collective-permute-start.6 = (bf16[1,4,8,256]{3,2,1,0:T(8,128)(2,1)S(1)}, bf16[1,4,8,256]{3,2,1,0:T(8,128)(2,1)S(1)}, u32[]{:S(2)}, u32[]{:S(2)}) collective-permute-start(bf16[1,4,8,256]{3,2,1,0:T(8,128)(2,1)S(1)} %get-tuple-element.42), channel_id=1, source_target_pairs={{8,0},{16,8},{24,16},{32,24},{40,32},{48,40},{56,48},{64,56},{72,6... | collective-permute-start | bytes 49160 | tf_op jit(solution)/shard_map/ppermute | solution.py:23
  22.3 44.9 %all-to-all-start = ((f32[32,1,3,512]{3,1,2,0:T(1,128)}), f32[32,1,3,512]{3,1,2,0:T(1,128)S(1)}, u32[]{:S(2)}, u32[]{:S(2)}) async-start(f32[32,1,3,512]{3,1,2,0:T(1,128)} %broadcast_in_dim.9), calls=%async_computation | async-start | bytes 393216 | tf_op jit(solution)/shard_map/all_to_all | solution.py:30
  51.9 9.3 %collective-permute-start.8 = (bf16[4,1,8,256]{3,2,1,0:T(8,128)(2,1)S(1)}, bf16[4,1,8,256]{3,2,1,0:T(8,128)(2,1)S(1)}, u32[]{:S(2)}, u32[]{:S(2)}) collective-permute-start(bf16[4,1,8,256]{3,2,1,0:T(8,128)(2,1)S(1)} %get-tuple-element.35), channel_id=1, source_target_pairs={{1,0},{2,1},{3,2},{4,3},{5,4},{6,5},{7,6},{9,8},{10,9},{11,10},{12... | collective-permute-start | bytes 49160 | tf_op jit(solution)/shard_map/ppermute | solution.py:23
  53.2 8.1 %collective-permute-start.7 = (bf16[4,1,8,256]{3,2,1,0:T(8,128)(2,1)S(1)}, bf16[4,1,8,256]{3,2,1,0:T(8,128)(2,1)S(1)}, u32[]{:S(2)}, u32[]{:S(2)}) collective-permute-start(bf16[4,1,8,256]{3,2,1,0:T(8,128)(2,1)S(1)} %get-tuple-element.36), channel_id=1, source_target_pairs={{0,1},{1,2},{2,3},{3,4},{4,5},{5,6},{6,7},{8,9},{9,10},{10,11},{11... | collective-permute-start | bytes 49160 | tf_op jit(solution)/shard_map/ppermute | solution.py:20
  56.3 10.8 %collective-permute-start.4 = (f32[6,2,512]{2,1,0:T(2,128)S(1)}, f32[6,2,512]{2,1,0:T(2,128)S(1)}, u32[]{:S(2)}, u32[]{:S(2)}) collective-permute-start(f32[6,2,512]{2,1,0:T(2,128)S(1)} %get-tuple-element.39), channel_id=1, source_target_pairs={{1,0},{2,1},{3,2},{4,3},{5,4},{6,5},{7,6},{9,8},{10,9},{11,10},{12... | collective-permute-start | bytes 73736 | tf_op jit(solution)/shard_map/ppermute | solution.py:23
  57.6 9.5 %collective-permute-start.3 = (f32[6,2,512]{2,1,0:T(2,128)S(1)}, f32[6,2,512]{2,1,0:T(2,128)S(1)}, u32[]{:S(2)}, u32[]{:S(2)}) collective-permute-start(f32[6,2,512]{2,1,0:T(2,128)S(1)} %get-tuple-element.40), channel_id=1, source_target_pairs={{0,1},{1,2},{2,3},{3,4},{4,5},{5,6},{6,7},{8,9},{9,10},{10,11},{11... | collective-permute-start | bytes 73736 | tf_op jit(solution)/shard_map/ppermute | solution.py:20
  68.6 26.9 %all-to-all-start.1 = ((f32[8,32,1,3,512]{4,1,3,2,0:T(8,128)}), f32[8,32,1,3,512]{4,1,3,2,0:T(8,128)S(1)}, u32[]{:S(2)}, u32[]{:S(2)}) async-start(f32[8,32,1,3,512]{4,1,3,2,0:T(8,128)} %broadcast_in_dim.22), calls=%async_computation.1 | async-start | bytes 3145728 | tf_op jit(solution)/shard_map/all_to_all | solution.py:30
  98.9 6.1 %copy-start.1 = (bf16[2,64,27,64]{3,2,1,0:T(8,128)(2,1)S(1)}, bf16[2,64,27,64]{3,2,1,0:T(8,128)(2,1)}, u32[]{:S(2)}) copy-start(bf16[2,64,27,64]{3,2,1,0:T(8,128)(2,1)} %reshape.132) | copy-start | bytes 1327108
  98.9 9.2 %copy-start.3 = (bf16[2,4,64,64]{3,2,1,0:T(8,128)(2,1)S(1)}, bf16[2,4,64,64]{3,2,1,0:T(8,128)(2,1)}, u32[]{:S(2)}) copy-start(bf16[2,4,64,64]{3,2,1,0:T(8,128)(2,1)} %param.14) | copy-start | bytes 196612
  99.6 9.7 %copy-start.4 = (f32[2,4,8,256,1]{3,2,0,1,4:T(8,128)S(1)}, f32[2,4,8,256,1]{3,2,0,1,4:T(8,128)}, u32[]{:S(2)}) copy-start(f32[2,4,8,256,1]{3,2,0,1,4:T(8,128)} %fusion) | copy-start | bytes 196612
  99.6 10.0 %copy-start.5 = (s32[2,4,256]{2,1,0:T(4,128)S(1)}, s32[2,4,256]{2,1,0:T(4,128)}, u32[]{:S(2)}) copy-start(s32[2,4,256]{2,1,0:T(4,128)} %param.10) | copy-start | bytes 24580
  103.6 3.6 %collective-permute-start = (f32[8,64]{1,0:T(8,128)S(1)}, f32[8,64]{1,0:T(8,128)S(1)}, u32[]{:S(2)}, u32[]{:S(2)}) collective-permute-start(f32[8,64]{1,0:T(8,128)S(1)} %convolution_bitcast_fusion.4), channel_id=1, source_target_pairs={{0,8},{8,0},{16,24},{24,16},{32,40},{40,32},{48,56},{56,48},{64,72... | collective-permute-start | bytes 6152 | tf_op jit(solution)/shard_map/ppermute | solution.py:56
where the time goes:
time: 112 us; the launch traced here: 111 us
  starting transfers between devices  40.7 us (36%)
  local copies, waits for them, and re-layouts  32.3 us (29%)
  matrix products  22.1 us (20%)
  waiting for transfers between devices  14 us (12%)
  other arithmetic  1.42 us (1%)
    ppermute x4, starting transfers between devices, with_halo(): lax.ppermute(lax.slice_in_dim(block, 0, width, axis=dim), axis, backward)  16.3 us
    all_to_all x2, waiting for transfers between devices, copy_for_each(): lax.all_to_all(jnp.broadcast_to(value[None], (length, *value.shape)), axi...  12.9 us
    unnamed x22, local copies, waits for them, and re-layouts  12.7 us
    all_to_all x2, starting transfers between devices, copy_for_each(): lax.all_to_all(jnp.broadcast_to(value[None], (length, *value.shape)), axi...  12.4 us
    ppermute x4, starting transfers between devices, with_halo(): lax.ppermute(lax.slice_in_dim(block, block.shape[dim] - width, None, axis...  10.5 us
    dot_general x1, matrix products, body(): jnp.einsum('wuvtsj,uwvktj->uwvsk', leaf_sources, leaf_couplings, precisio...  6.76 us
    dot_general x1, matrix products, body(): jnp.einsum('ucqsp,ucaqp->ucsa', neighbours, blocks, preferred_element_typ...  5.64 us
    reshape x1, local copies, waits for them, and re-layouts, body(): leaf_couplings = leaf_coupling.reshape(2, 2, 2, rank_size, 27, rank_size)  5 us
  transfers between devices with their start and end apart: 11, of which 2 were waited for; matrix products, arithmetic and copies ran while one was open for 37% of the time, Pallas kernels for 0%

commit v1 on v0

v1 whole, which is shorter than its diff:
```python
import functools

import jax
import jax.numpy as jnp
from jax import lax
from jax.experimental import pallas as pl
from jax.experimental.pallas import tpu as pltpu
from jax.sharding import PartitionSpec as P

MESH = pl.DeviceIdType.MESH
F32 = jnp.float32
BF16 = jnp.bfloat16


def dot_nt(a, b):
    return lax.dot_general(a, b, (((1,), (1,)), ((), ())), preferred_element_type=F32)


def dot_nn(a, b):
    return lax.dot_general(a, b, (((1,), (0,)), ((), ())), preferred_element_type=F32)


def split(x):
    high = x.astype(BF16).astype(F32)
    return jnp.concatenate([high, x - high], axis=0).astype(BF16)


def joined(out, at=0):
    return out[at : at + 8] + out[at + 8 : at + 16]


def list_positions(u, v):
    return [
        (a, b) for a in range(6) for b in range(6) if max(abs(a - 2 - u), abs(b - 2 - v)) > 1
    ]


def low_lanes(shape):
    return lax.broadcasted_iota(jnp.int32, shape, len(shape) - 1) % 128 < 64


def listed(tiles, swapped, u, v, low):
    where = list_positions(u, v)
    pieces = []
    for i in range(14):
        a, b = where[2 * i]
        first = tiles[a][b // 2] if b % 2 == 0 else swapped[a][b // 2]
        if 2 * i + 1 == len(where):
            pieces.append(first[:, :64])
            continue
        a2, b2 = where[2 * i + 1]
        second = tiles[a2][b2 // 2] if b2 % 2 == 1 else swapped[a2][b2 // 2]
        if first is second:
            pieces.append(first)
        else:
            pieces.append(jnp.where(low, first, second))
    return pieces


def kernel(
    rs_h, order_h, basis_h, near_h, lcp_h, t_h, bcp_h, bt_h, ccp_h,
    out_ref,
    rs, order, basis, near, lcp, tr, bcp, bt, ccp,
    sel, tcat, ohalo, lwin, bwin, pack, row, coarse, half, other_half,
    acc, basis_in,
    load_sem, near_sem,
    p1_send, p1_recv, p2_send, p2_recv,
    o_send, o_recv, l_send, l_recv, b_send, b_recv, x_send, x_recv,
):
    gx = lax.axis_index("gx")
    gy = lax.axis_index("gy")
    y, z = gx // 8, gx % 8
    x, c = gy // 2, gy % 2
    pair, u = gx // 2, gx % 2

    loads = [
        pltpu.make_async_copy(src, dst, load_sem.at[i])
        for i, (src, dst) in enumerate(
            [
                (order_h, order), (rs_h, rs), (basis_h, basis), (t_h, tr), (bt_h, bt),
                (lcp_h, lcp), (bcp_h, bcp), (ccp_h, ccp),
            ]
        )
    ]
    near_loads = [
        pltpu.make_async_copy(near_h.at[i // 4, i % 4], near.at[i], near_sem.at[i])
        for i in range(8)
    ]
    for copy in loads[:5]:
        copy.start()
    for copy in near_loads:
        copy.start()
    for copy in loads[5:]:
        copy.start()

    barrier = pltpu.get_barrier_semaphore()

    def tell(to_gx, to_gy):
        pl.semaphore_signal(barrier, inc=1, device_id=(to_gx, to_gy), device_id_type=MESH)

    own = z * 2 + c
    flip = z + 1 - 2 * (z % 2)
    for d in range(1, 16):
        t = (own + d) % 16
        tell(8 * y + t // 2, 2 * x + t % 2)
    half_id = z % 2
    keeps = y // 2 == half_id
    for j in range(2):
        for dx in range(4):
            from_y = 2 * half_id + (y + j) % 2
            from_z = z if j == 0 else flip
            from_x = (x + 4 - dx) % 4
            if j == 0 and dx == 0:

                @pl.when(jnp.logical_not(keeps))
                def _():
                    tell(8 * from_y + from_z, 2 * from_x + c)
            else:
                tell(8 * from_y + from_z, 2 * from_x + c)
    left, right = (gy + 7) % 8, (gy + 1) % 8
    tell(gx, left)
    tell(gx, right)
    up, down = (gx + 31) % 32, (gx + 1) % 32
    pair_rows = [(pair + 15) % 16, (pair + 1) % 16]
    for other_pair in pair_rows:
        for ut in range(2):
            tell(2 * other_pair + ut, gy)
    partner = 2 * pair + 1 - u
    tell(partner, gy)

    low8 = low_lanes((8, 128))
    low4 = low_lanes((4, 128))

    loads[0].wait()
    loads[1].wait()
    places = lax.broadcasted_iota(jnp.int32, (256, 256), 0)
    ordered = []
    for i in range(8):
        r, k = i // 4, i % 4
        chosen = (places == order[r, k : k + 1, :]).astype(F32).astype(BF16)
        sel[i] = chosen
        points = dot_nn(rs[r, k], chosen)
        ordered.append(points)
        ohalo[1 + r, 1 + k] = points.astype(BF16)
    loads[2].wait()
    tiles = {}
    for r in range(2):
        for w in range(2):
            both = jnp.concatenate([ordered[4 * r + 2 * w], ordered[4 * r + 2 * w + 1]], 0)
            out = dot_nt(both.astype(BF16), basis[r, 2 * w : 2 * w + 2].reshape(128, 256))
            tiles[r, w] = jnp.where(low8, out[:8], out[8:])
            lwin[2 + r, 1 + w] = tiles[r, w]
    loads[3].wait()
    for w in range(2):
        for r in range(2):
            for v in range(2):
                at = (2 * r + v) * 64
                tcat[at : at + 64, 64 * w : 64 * w + 64] = tr[r, 2 * w + v]
    stacked = [split(jnp.concatenate([tiles[0, w], tiles[1, w]], 1)) for w in range(2)]
    out = dot_nn(jnp.concatenate(stacked, 0), tcat[...])
    box = jnp.where(low8, joined(out, 0), joined(out, 16))
    bwin[2 + u, 1] = box
    loads[4].wait()
    bt_all = bt[0].reshape(128, 64)
    part = joined(dot_nn(split(box), jnp.concatenate([bt_all, bt_all], 1)))
    pack[own] = jnp.where(low4, part[:4], part[4:])

    pl.semaphore_wait(barrier, jnp.where(keeps, 29, 30))

    sends = []
    stage1 = []
    for d in range(1, 16):
        t = (own + d) % 16
        copy = pltpu.make_async_remote_copy(
            pack.at[own], pack.at[own], p1_send.at[d - 1], p1_recv.at[d - 1],
            device_id=(8 * y + t // 2, 2 * x + t % 2), device_id_type=MESH,
        )
        copy.start()
        stage1.append(copy)
    column = []

    def send(group, src, dst, ssem, rsem, to):
        copy = pltpu.make_async_remote_copy(
            src, dst, ssem, rsem, device_id=to, device_id_type=MESH
        )
        copy.start()
        group.append(copy)

    own_rows = pl.ds(1, 2)
    send(column, ohalo.at[own_rows, 4], ohalo.at[own_rows, 0], o_send.at[0], o_recv.at[0], (gx, right))
    send(column, ohalo.at[own_rows, 1], ohalo.at[own_rows, 5], o_send.at[1], o_recv.at[1], (gx, left))
    mid = pl.ds(2, 2)
    send(column, lwin.at[mid, 2], lwin.at[mid, 0], l_send.at[0], l_recv.at[0], (gx, right))
    send(column, lwin.at[mid, 1], lwin.at[mid, 3], l_send.at[1], l_recv.at[1], (gx, left))
    send(column, bwin.at[2 + u, 1], bwin.at[2 + u, 0], b_send.at[0], b_recv.at[6], (gx, right))
    send(column, bwin.at[2 + u, 1], bwin.at[2 + u, 2], b_send.at[1], b_recv.at[7], (gx, left))

    def near_terms(i, inside):
        r, k = i // 4, i % 4
        total = None
        for a in (-1, 0, 1):
            for b in (-1, 0, 1):
                if (0 <= r + a < 2 and 0 <= k + b < 4) != inside:
                    continue
                q = 3 * (a + 1) + b + 1
                term = dot_nt(
                    ohalo[1 + r + a, 1 + k + b], near[i, :, q * 256 : (q + 1) * 256]
                )
                total = term if total is None else total + term
        return total

    for i in range(4):
        near_loads[i].wait()
        acc[i] = near_terms(i, True)

    for copy in stage1:
        copy.wait_recv()
    for zp in range(4):
        pairs = [pack[4 * zp + k] + pack[4 * zp + 2 + k] for k in range(2)]
        turned = [pltpu.roll(p, 64, 1) for p in pairs]
        row[zp] = jnp.concatenate(
            [jnp.where(low4, pairs[0], turned[1]), jnp.where(low4, turned[0], pairs[1])], 0
        )
    my_half = y // 2
    odd = jnp.where(z % 2 == my_half, 0, 1)
    to_z = z + odd * (1 - 2 * (z % 2))
    slot = (y % 2) * 4 + x
    stage2 = []
    for i in range(2):
        for dx in range(4):
            to_y = (y + 2 * i + odd) % 4
            to_x = (x + dx) % 4
            copy = pltpu.make_async_remote_copy(
                row, coarse.at[pl.ds((y % 2) * 4, 4), x],
                p2_send.at[4 * i + dx], p2_recv.at[slot],
                device_id=(8 * to_y + to_z, 2 * to_x + c), device_id_type=MESH,
            )
            stage2.append(copy)
            if i == 0 and dx == 0:

                @pl.when(odd == 1)
                def _():
                    copy.start()

                @pl.when(odd == 0)
                def _():
                    pltpu.make_async_copy(
                        row, coarse.at[pl.ds((y % 2) * 4, 4), x], p2_recv.at[slot]
                    ).start()
            else:
                copy.start()

    for copy in column:
        copy.wait()

    @pl.when(gy == 0)
    def _():
        ohalo[1:3, 0] = jnp.zeros((2, 8, 256), BF16)
        lwin[2:4, 0] = jnp.zeros((2, 8, 128), F32)
        bwin[2 + u, 0] = jnp.zeros((8, 128), F32)

    @pl.when(gy == 7)
    def _():
        ohalo[1:3, 5] = jnp.zeros((2, 8, 256), BF16)
        lwin[2:4, 3] = jnp.zeros((2, 8, 128), F32)
        bwin[2 + u, 2] = jnp.zeros((8, 128), F32)

    rows = []
    send(rows, ohalo.at[2], ohalo.at[0], o_send.at[2], o_recv.at[2], (down, gy))
    send(rows, ohalo.at[1], ohalo.at[3], o_send.at[3], o_recv.at[3], (up, gy))
    send(rows, lwin.at[mid], lwin.at[pl.ds(0, 2)], l_send.at[2], l_recv.at[2], (down, gy))
    send(rows, lwin.at[mid], lwin.at[pl.ds(4, 2)], l_send.at[3], l_recv.at[3], (up, gy))
    box_rows = []
    for which, base in ((0, 4), (1, 0)):
        for ut in range(2):
            send(
                box_rows, bwin.at[2 + u], bwin.at[base + u],
                b_send.at[2 + 2 * which + ut], b_recv.at[base + u],
                (2 * pair_rows[which] + ut, gy),
            )
    send(
        box_rows, bwin.at[2 + u], bwin.at[2 + u], b_send.at[6], b_recv.at[2 + u], (partner, gy)
    )

    for i in range(4, 8):
        near_loads[i].wait()
        acc[i] = near_terms(i, True)

    for copy in rows:
        copy.wait()
    for a in (0, 1, 4, 5):
        pltpu.make_async_copy(bwin.at[a], bwin.at[a], b_recv.at[a]).wait()
    pltpu.make_async_copy(bwin.at[3 - u], bwin.at[3 - u], b_recv.at[3 - u]).wait()
    for copy in box_rows:
        copy.wait_send()

    @pl.when(gx == 0)
    def _():
        ohalo[0] = jnp.zeros((6, 8, 256), BF16)
        lwin[0:2] = jnp.zeros((2, 4, 8, 128), F32)

    @pl.when(gx == 31)
    def _():
        ohalo[3] = jnp.zeros((6, 8, 256), BF16)
        lwin[4:6] = jnp.zeros((2, 4, 8, 128), F32)

    @pl.when(pair == 0)
    def _():
        bwin[0:2] = jnp.zeros((2, 3, 8, 128), F32)

    @pl.when(pair == 15)
    def _():
        bwin[4:6] = jnp.zeros((2, 3, 8, 128), F32)

    for i in range(8):
        r, k = i // 4, i % 4
        total = acc[i] + near_terms(i, False)
        both = jnp.concatenate([basis[r, k], split(total)], 0)
        moved = dot_nt(both, sel[i])
        basis_in[i] = moved[:64].astype(BF16)
        acc[i] = joined(moved, 64)

    loads[5].wait()
    leaf_tiles = [[lwin[a, j] for j in range(4)] for a in range(6)]
    leaf_turned = [[pltpu.roll(t, 64, 1) for t in line] for line in leaf_tiles]
    leaf_far = {}
    for r in range(2):
        for w in range(2):
            here = [line[w : w + 3] for line in leaf_tiles]
            here_turned = [line[w : w + 3] for line in leaf_turned]
            both = [
                split(jnp.concatenate(listed(here, here_turned, r, v, low8), 1))
                for v in range(2)
            ]
            out = dot_nt(
                jnp.concatenate(both, 0), lcp[r, 2 * w : 2 * w + 2].reshape(128, 1728)
            )
            leaf_far[r, w] = jnp.where(low8, joined(out, 0), joined(out, 16))
    loads[6].wait()
    box_tiles = [[bwin[a, j] for j in range(3)] for a in range(6)]
    box_turned = [[pltpu.roll(t, 64, 1) for t in line] for line in box_tiles]
    both = []
    for v in range(2):
        even = jnp.concatenate(listed(box_tiles, box_turned, 0, v, low8), 1)
        odds = jnp.concatenate(listed(box_tiles, box_turned, 1, v, low8), 1)
        both.append(split(jnp.where(u == 0, even, odds)))
    out = dot_nt(jnp.concatenate(both, 0), bcp[0].reshape(128, 1728))
    box_far = jnp.where(low8, joined(out, 0), joined(out, 16))

    loads[7].wait()
    for i in range(8):
        pltpu.make_async_copy(row, coarse.at[pl.ds(0, 4), 0], p2_recv.at[i]).wait()
    lane = lax.broadcasted_iota(jnp.int32, (8, 128), 1)
    near_cols = []
    for xs in range(4):
        apart = 2 * xs + lane // 64 - gy
        near_cols.append((apart >= -1) & (apart <= 1))
    sources = []
    for i in range(8):
        apart = 8 * half_id + i - pair
        near_row = (apart >= -1) & (apart <= 1)
        for xs in range(4):
            sources.append(jnp.where(near_cols[xs] & near_row, 0.0, coarse[i, xs]))
    mine = joined(dot_nt(split(jnp.concatenate(sources, 1)), ccp[0, 0]))
    half[...] = mine
    swap = pltpu.make_async_remote_copy(
        half, other_half, x_send.at[0], x_recv.at[0], device_id=(partner, gy), device_id_type=MESH
    )
    swap.start()
    for copy in stage1:
        copy.wait_send()
    for n, copy in enumerate(stage2):
        if n == 0:

            @pl.when(odd == 1)
            def _():
                copy.wait_send()
        else:
            copy.wait_send()
    swap.wait()

    coarse_far = mine + other_half[...]
    box_down = joined(dot_nt(split(coarse_far), bt_all)) + box_far
    both = [split(jnp.where(low8, box_down, 0.0)), split(jnp.where(low8, 0.0, box_down))]
    out = dot_nt(jnp.concatenate(both, 0), tcat[...])
    for r in range(2):
        for w in range(2):
            leaf_down = joined(out[:, 128 * r : 128 * r + 128], 16 * w) + leaf_far[r, w]
            both = [split(jnp.where(low8, leaf_down, 0.0)), split(jnp.where(low8, 0.0, leaf_down))]
            i = 4 * r + 2 * w
            last = dot_nn(jnp.concatenate(both, 0), basis_in[i : i + 2].reshape(128, 256))
            for v in range(2):
                out_ref[r, 2 * w + v] = joined(last, 16 * v) + acc[i + v]


def body(rs, order, basis, near, lcp, tr, bcp, bt, ccp):
    hbm = pl.BlockSpec(memory_space=pltpu.HBM)
    dma = pltpu.SemaphoreType.DMA
    return pl.pallas_call(
        kernel,
        out_shape=jax.ShapeDtypeStruct((2, 4, 8, 256), F32),
        in_specs=[hbm] * 9,
        out_specs=pl.BlockSpec(memory_space=pltpu.VMEM),
        scratch_shapes=[
            pltpu.VMEM(rs.shape, BF16),
            pltpu.VMEM(order.shape, jnp.int32),
            pltpu.VMEM(basis.shape, BF16),
            pltpu.VMEM((8, 256, 2304), BF16),
            pltpu.VMEM(lcp.shape, BF16),
            pltpu.VMEM(tr.shape, BF16),
            pltpu.VMEM(bcp.shape, BF16),
            pltpu.VMEM(bt.shape, BF16),
            pltpu.VMEM(ccp.shape, BF16),
            pltpu.VMEM((8, 256, 256), BF16),
            pltpu.VMEM((256, 128), BF16),
            pltpu.VMEM((4, 6, 8, 256), BF16),
            pltpu.VMEM((6, 4, 8, 128), F32),
            pltpu.VMEM((6, 3, 8, 128), F32),
            pltpu.VMEM((16, 4, 128), F32),
            pltpu.VMEM((4, 8, 128), F32),
            pltpu.VMEM((8, 4, 8, 128), F32),
            pltpu.VMEM((8, 64), F32),
            pltpu.VMEM((8, 64), F32),
            pltpu.VMEM((8, 8, 256), F32),
            pltpu.VMEM((8, 64, 256), BF16),
            dma((8,)),
            dma((8,)),
            dma((15,)),
            dma((15,)),
            dma((8,)),
            dma((8,)),
            dma((4,)),
            dma((4,)),
            dma((4,)),
            dma((4,)),
            dma((7,)),
            dma((8,)),
            dma((1,)),
            dma((1,)),
        ],
        compiler_params=pltpu.CompilerParams(
            collective_id=0, has_side_effects=True, vmem_limit_bytes=56 * 2**20
        ),
    )(rs, order, basis, near, lcp, tr, bcp, bt, ccp)


def solution(mesh):
    four = P("gx", "gy", None, None)
    placed = (four, P("gx", "gy", None)) + (four,) * 7
    return jax.shard_map(body, mesh=mesh, in_specs=placed, out_specs=four, check_vma=False)
```

time: 112 us -> 33.3 us (0.30)
  the two profiles are of different devices: /device:TPU:8 before, /device:TPU:4 now
where the time goes in v1:
time: 33.3 us; the launch traced here: 33.2 us
  Pallas kernels  31.7 us (95%)
  local copies, waits for them, and re-layouts  1.47 us (4%)
    pallas_call x1, Pallas kernels, body(): pl.pallas_call(kernel, out_shape=jax.ShapeDtypeStruct((2, 4, 8, 256), F32...  31.7 us
    unnamed x1, local copies, waits for them, and re-layouts  1.47 us

profile of v1, /device:TPU:4, one launch (start us, length us, event | category | flops | bytes accessed | tf_op | source)
XLA Modules:
  0.0 33.2 jit_solution(6660854290845814677)
XLA Ops:
  0.0 31.7 %shard_map.91 = f32[2,4,8,256]{3,2,1,0:T(8,128)} custom-call(bf16[2,4,8,256]{3,2,1,0:T(8,128)(2,1)} %rs_h.1, s32[2,4,256]{2,1,0:T(4,128)} %order_h.1, bf16[2,4,64,256]{3,2,1,0:T(8,128)(2,1)} %basis_h.1, bf16[2,4,256,2304]{3,2,1,0:T(8,128)(2,1)} %near_h.1, bf16[2,4,64,1728]{3,2,1,0:T(8,128)(2,1)} %lcp_h.1, bf16[2,4,64,64]{3,2,1,0:T(8,128)(2,1)} %t_h.1, ...), custom_call_target="tpu_custom_call" | custom-call | tf_op jit(solution)/shard_map/pallas_call | solution.py:399
  31.7 1.5 %copy.11 = f32[2,4,8,256]{3,2,1,0:T(8,128)} copy(f32[2,4,8,256]{3,2,1,0:T(8,128)} %shard_map.91) | data formatting | bytes 131072

commit v2 on v1

--- a/solution.py
+++ b/solution.py
@@ -88,10 +88,6 @@
     ]
     for copy in loads[:5]:
         copy.start()
-    for copy in near_loads:
-        copy.start()
-    for copy in loads[5:]:
-        copy.start()
 
     barrier = pltpu.get_barrier_semaphore()
 
@@ -100,13 +96,14 @@
 
     own = z * 2 + c
     flip = z + 1 - 2 * (z % 2)
-    for d in range(1, 16):
+    half_id = z % 2
+    keeps = y // 2 == half_id
+    far_first = sorted(range(1, 16), key=lambda d: abs(d - 8))
+    for d in far_first:
         t = (own + d) % 16
         tell(8 * y + t // 2, 2 * x + t % 2)
-    half_id = z % 2
-    keeps = y // 2 == half_id
-    for j in range(2):
-        for dx in range(4):
+    for dx in (2, 1, 3, 0):
+        for j in range(2):
             from_y = 2 * half_id + (y + j) % 2
             from_z = z if j == 0 else flip
             from_x = (x + 4 - dx) % 4
@@ -118,15 +115,23 @@
             else:
                 tell(8 * from_y + from_z, 2 * from_x + c)
     left, right = (gy + 7) % 8, (gy + 1) % 8
-    tell(gx, left)
-    tell(gx, right)
     up, down = (gx + 31) % 32, (gx + 1) % 32
-    pair_rows = [(pair + 15) % 16, (pair + 1) % 16]
-    for other_pair in pair_rows:
+    partner = 2 * pair + 1 - u
+    targets = []
+    for step in (-1, 1, 0):
         for ut in range(2):
-            tell(2 * other_pair + ut, gy)
-    partner = 2 * pair + 1 - u
-    tell(partner, gy)
+            to_gx = partner if step == 0 else 2 * ((pair + 16 + step) % 16) + ut
+            if step == 0 and ut == 1:
+                continue
+            for to_gy, column in ((left, 2), (gy, 1), (right, 0)):
+                targets.append((step, to_gx, to_gy, column))
+    targets += [(None, gx, left, 2), (None, gx, right, 0)]
+    for _, to_gx, to_gy, _ in targets:
+        tell(to_gx, to_gy)
+    for copy in near_loads:
+        copy.start()
+    for copy in loads[5:]:
+        copy.start()
 
     low8 = low_lanes((8, 128))
     low4 = low_lanes((4, 128))
@@ -165,35 +170,53 @@
     part = joined(dot_nn(split(box), jnp.concatenate([bt_all, bt_all], 1)))
     pack[own] = jnp.where(low4, part[:4], part[4:])
 
-    pl.semaphore_wait(barrier, jnp.where(keeps, 29, 30))
+    pl.semaphore_wait(barrier, jnp.where(keeps, 39, 40))
 
     sends = []
-    stage1 = []
-    for d in range(1, 16):
-        t = (own + d) % 16
-        copy = pltpu.make_async_remote_copy(
-            pack.at[own], pack.at[own], p1_send.at[d - 1], p1_recv.at[d - 1],
-            device_id=(8 * y + t // 2, 2 * x + t % 2), device_id_type=MESH,
-        )
-        copy.start()
-        stage1.append(copy)
-    column = []
-
-    def send(group, src, dst, ssem, rsem, to):
+
+    def send(src, dst, ssem, rsem, to):
         copy = pltpu.make_async_remote_copy(
             src, dst, ssem, rsem, device_id=to, device_id_type=MESH
         )
         copy.start()
-        group.append(copy)
-
-    own_rows = pl.ds(1, 2)
-    send(column, ohalo.at[own_rows, 4], ohalo.at[own_rows, 0], o_send.at[0], o_recv.at[0], (gx, right))
-    send(column, ohalo.at[own_rows, 1], ohalo.at[own_rows, 5], o_send.at[1], o_recv.at[1], (gx, left))
-    mid = pl.ds(2, 2)
-    send(column, lwin.at[mid, 2], lwin.at[mid, 0], l_send.at[0], l_recv.at[0], (gx, right))
-    send(column, lwin.at[mid, 1], lwin.at[mid, 3], l_send.at[1], l_recv.at[1], (gx, left))
-    send(column, bwin.at[2 + u, 1], bwin.at[2 + u, 0], b_send.at[0], b_recv.at[6], (gx, right))
-    send(column, bwin.at[2 + u, 1], bwin.at[2 + u, 2], b_send.at[1], b_recv.at[7], (gx, left))
+        sends.append(copy)
+
+    for n, d in enumerate(far_first):
+        t = (own + d) % 16
+        send(
+            pack.at[own], pack.at[own], p1_send.at[n], p1_recv.at[0],
+            (8 * y + t // 2, 2 * x + t % 2),
+        )
+    mine, mid, cols = pl.ds(1, 2), pl.ds(2, 2), pl.ds(1, 4)
+    above, below, pairs2 = pl.ds(0, 2), pl.ds(4, 2), pl.ds(1, 2)
+    for n, (src, dst, rsem, to) in enumerate([
+        (ohalo.at[2, cols], ohalo.at[0, cols], 0, (down, gy)),
+        (ohalo.at[1, cols], ohalo.at[3, cols], 1, (up, gy)),
+        (ohalo.at[2, 4], ohalo.at[0, 0], 0, (down, right)),
+        (ohalo.at[2, 1], ohalo.at[0, 5], 0, (down, left)),
+        (ohalo.at[1, 4], ohalo.at[3, 0], 1, (up, right)),
+        (ohalo.at[1, 1], ohalo.at[3, 5], 1, (up, left)),
+        (ohalo.at[mine, 4], ohalo.at[mine, 0], 2, (gx, right)),
+        (ohalo.at[mine, 1], ohalo.at[mine, 5], 3, (gx, left)),
+    ]):
+        send(src, dst, o_send.at[n], o_recv.at[rsem], to)
+    for n, (src, dst, rsem, to) in enumerate([
+        (lwin.at[mid, pairs2], lwin.at[above, pairs2], 0, (down, gy)),
+        (lwin.at[mid, pairs2], lwin.at[below, pairs2], 1, (up, gy)),
+        (lwin.at[mid, 2], lwin.at[above, 0], 0, (down, right)),
+        (lwin.at[mid, 1], lwin.at[above, 3], 0, (down, left)),
+        (lwin.at[mid, 2], lwin.at[below, 0], 1, (up, right)),
+        (lwin.at[mid, 1], lwin.at[below, 3], 1, (up, left)),
+        (lwin.at[mid, 2], lwin.at[mid, 0], 2, (gx, right)),
+        (lwin.at[mid, 1], lwin.at[mid, 3], 3, (gx, left)),
+    ]):
+        send(src, dst, l_send.at[n], l_recv.at[rsem], to)
+    for n, (step, to_gx, to_gy, column) in enumerate(targets):
+        slot = 2 + u if step is None else 2 - 2 * step + u
+        send(
+            bwin.at[2 + u, 1], bwin.at[slot, column], b_send.at[n], b_recv.at[slot],
+            (to_gx, to_gy),
+        )
 
     def near_terms(i, inside):
         r, k = i // 4, i % 4
@@ -209,12 +232,13 @@
                 total = term if total is None else total + term
         return total
 
-    for i in range(4):
+    for i in range(8):
         near_loads[i].wait()
         acc[i] = near_terms(i, True)
-
-    for copy in stage1:
-        copy.wait_recv()
+        basis_in[i] = dot_nt(basis[i // 4, i % 4], sel[i]).astype(BF16)
+
+    arrived = pack.at[pl.ds(0, 15)]
+    pltpu.make_async_copy(arrived, arrived, p1_recv.at[0]).wait()
     for zp in range(4):
         pairs = [pack[4 * zp + k] + pack[4 * zp + 2 + k] for k in range(2)]
         turned = [pltpu.roll(p, 64, 1) for p in pairs]
@@ -224,7 +248,6 @@
     my_half = y // 2
     odd = jnp.where(z % 2 == my_half, 0, 1)
     to_z = z + odd * (1 - 2 * (z % 2))
-    slot = (y % 2) * 4 + x
     stage2 = []
     for i in range(2):
         for dx in range(4):
@@ -232,7 +255,7 @@
             to_x = (x + dx) % 4
             copy = pltpu.make_async_remote_copy(
                 row, coarse.at[pl.ds((y % 2) * 4, 4), x],
-                p2_send.at[4 * i + dx], p2_recv.at[slot],
+                p2_send.at[4 * i + dx], p2_recv.at[0],
                 device_id=(8 * to_y + to_z, 2 * to_x + c), device_id_type=MESH,
             )
             stage2.append(copy)
@@ -245,54 +268,38 @@
                 @pl.when(odd == 0)
                 def _():
                     pltpu.make_async_copy(
-                        row, coarse.at[pl.ds((y % 2) * 4, 4), x], p2_recv.at[slot]
+                        row, coarse.at[pl.ds((y % 2) * 4, 4), x], p2_recv.at[0]
                     ).start()
             else:
                 copy.start()
 
-    for copy in column:
-        copy.wait()
+    def arrive(ref, sem):
+        pltpu.make_async_copy(ref, ref, sem).wait()
+
+    arrive(ohalo.at[0], o_recv.at[0])
+    arrive(ohalo.at[3], o_recv.at[1])
+    arrive(ohalo.at[mine, 0], o_recv.at[2])
+    arrive(ohalo.at[mine, 5], o_recv.at[3])
+    arrive(lwin.at[above], l_recv.at[0])
+    arrive(lwin.at[below], l_recv.at[1])
+    arrive(lwin.at[mid, 0], l_recv.at[2])
+    arrive(lwin.at[mid, 3], l_recv.at[3])
+    for a in (0, 1, 4, 5):
+        arrive(bwin.at[a], b_recv.at[a])
+    arrive(bwin.at[3 - u], b_recv.at[3 - u])
+    arrive(bwin.at[2 + u, pl.ds(0, 2)], b_recv.at[2 + u])
 
     @pl.when(gy == 0)
     def _():
-        ohalo[1:3, 0] = jnp.zeros((2, 8, 256), BF16)
-        lwin[2:4, 0] = jnp.zeros((2, 8, 128), F32)
-        bwin[2 + u, 0] = jnp.zeros((8, 128), F32)
+        ohalo[:, 0] = jnp.zeros((4, 8, 256), BF16)
+        lwin[:, 0] = jnp.zeros((6, 8, 128), F32)
+        bwin[:, 0] = jnp.zeros((6, 8, 128), F32)
 
     @pl.when(gy == 7)
     def _():
-        ohalo[1:3, 5] = jnp.zeros((2, 8, 256), BF16)
-        lwin[2:4, 3] = jnp.zeros((2, 8, 128), F32)
-        bwin[2 + u, 2] = jnp.zeros((8, 128), F32)
-
-    rows = []
-    send(rows, ohalo.at[2], ohalo.at[0], o_send.at[2], o_recv.at[2], (down, gy))
-    send(rows, ohalo.at[1], ohalo.at[3], o_send.at[3], o_recv.at[3], (up, gy))
-    send(rows, lwin.at[mid], lwin.at[pl.ds(0, 2)], l_send.at[2], l_recv.at[2], (down, gy))
-    send(rows, lwin.at[mid], lwin.at[pl.ds(4, 2)], l_send.at[3], l_recv.at[3], (up, gy))
-    box_rows = []
-    for which, base in ((0, 4), (1, 0)):
-        for ut in range(2):
-            send(
-                box_rows, bwin.at[2 + u], bwin.at[base + u],
-                b_send.at[2 + 2 * which + ut], b_recv.at[base + u],
-                (2 * pair_rows[which] + ut, gy),
-            )
-    send(
-        box_rows, bwin.at[2 + u], bwin.at[2 + u], b_send.at[6], b_recv.at[2 + u], (partner, gy)
-    )
-
-    for i in range(4, 8):
-        near_loads[i].wait()
-        acc[i] = near_terms(i, True)
-
-    for copy in rows:
-        copy.wait()
-    for a in (0, 1, 4, 5):
-        pltpu.make_async_copy(bwin.at[a], bwin.at[a], b_recv.at[a]).wait()
-    pltpu.make_async_copy(bwin.at[3 - u], bwin.at[3 - u], b_recv.at[3 - u]).wait()
-    for copy in box_rows:
-        copy.wait_send()
+        ohalo[:, 5] = jnp.zeros((4, 8, 256), BF16)
+        lwin[:, 3] = jnp.zeros((6, 8, 128), F32)
+        bwin[:, 2] = jnp.zeros((6, 8, 128), F32)
 
     @pl.when(gx == 0)
     def _():
@@ -313,12 +320,7 @@
         bwin[4:6] = jnp.zeros((2, 3, 8, 128), F32)
 
     for i in range(8):
-        r, k = i // 4, i % 4
-        total = acc[i] + near_terms(i, False)
-        both = jnp.concatenate([basis[r, k], split(total)], 0)
-        moved = dot_nt(both, sel[i])
-        basis_in[i] = moved[:64].astype(BF16)
-        acc[i] = joined(moved, 64)
+        acc[i] += near_terms(i, False)
 
     loads[5].wait()
     leaf_tiles = [[lwin[a, j] for j in range(4)] for a in range(6)]
@@ -348,8 +350,7 @@
     box_far = jnp.where(low8, joined(out, 0), joined(out, 16))
 
     loads[7].wait()
-    for i in range(8):
-        pltpu.make_async_copy(row, coarse.at[pl.ds(0, 4), 0], p2_recv.at[i]).wait()
+    arrive(coarse, p2_recv.at[0])
     lane = lax.broadcasted_iota(jnp.int32, (8, 128), 1)
     near_cols = []
     for xs in range(4):
@@ -361,13 +362,15 @@
         near_row = (apart >= -1) & (apart <= 1)
         for xs in range(4):
             sources.append(jnp.where(near_cols[xs] & near_row, 0.0, coarse[i, xs]))
-    mine = joined(dot_nt(split(jnp.concatenate(sources, 1)), ccp[0, 0]))
-    half[...] = mine
+    here = joined(dot_nt(split(jnp.concatenate(sources, 1)), ccp[0, 0]))
+    half[...] = here
     swap = pltpu.make_async_remote_copy(
         half, other_half, x_send.at[0], x_recv.at[0], device_id=(partner, gy), device_id_type=MESH
     )
     swap.start()
-    for copy in stage1:
+    for i in range(8):
+        acc[i] = joined(dot_nt(split(acc[i]), sel[i]))
+    for copy in sends:
         copy.wait_send()
     for n, copy in enumerate(stage2):
         if n == 0:
@@ -379,7 +382,7 @@
             copy.wait_send()
     swap.wait()
 
-    coarse_far = mine + other_half[...]
+    coarse_far = here + other_half[...]
     box_down = joined(dot_nt(split(coarse_far), bt_all)) + box_far
     both = [split(jnp.where(low8, box_down, 0.0)), split(jnp.where(low8, 0.0, box_down))]
     out = dot_nt(jnp.concatenate(both, 0), tcat[...])
@@ -426,15 +429,15 @@
             dma((8,)),
             dma((8,)),
             dma((15,)),
-            dma((15,)),
+            dma((1,)),
             dma((8,)),
+            dma((1,)),
             dma((8,)),
             dma((4,)),
+            dma((8,)),
             dma((4,)),
-            dma((4,)),
-            dma((4,)),
-            dma((7,)),
-            dma((8,)),
+            dma((17,)),
+            dma((6,)),
             dma((1,)),
             dma((1,)),
         ],

time: 33.3 us -> 26.1 us (0.78)
  the two profiles are of different devices: /device:TPU:4 before, /device:TPU:8 now
where the time goes in v2:
time: 26.1 us; the launch traced here: 25.9 us
  Pallas kernels  24.5 us (94%)
  local copies, waits for them, and re-layouts  1.47 us (6%)
    pallas_call x1, Pallas kernels, body(): pl.pallas_call(kernel, out_shape=jax.ShapeDtypeStruct((2, 4, 8, 256), F32...  24.5 us
    unnamed x1, local copies, waits for them, and re-layouts  1.47 us

profile of v2, /device:TPU:8, one launch (start us, length us, event | category | flops | bytes accessed | tf_op | source)
XLA Modules:
  0.0 25.9 jit_solution(1731374709023543052)
XLA Ops:
  0.0 24.5 %shard_map.91 = f32[2,4,8,256]{3,2,1,0:T(8,128)} custom-call(bf16[2,4,8,256]{3,2,1,0:T(8,128)(2,1)} %rs_h.1, s32[2,4,256]{2,1,0:T(4,128)} %order_h.1, bf16[2,4,64,256]{3,2,1,0:T(8,128)(2,1)} %basis_h.1, bf16[2,4,256,2304]{3,2,1,0:T(8,128)(2,1)} %near_h.1, bf16[2,4,64,1728]{3,2,1,0:T(8,128)(2,1)} %lcp_h.1, bf16[2,4,64,64]{3,2,1,0:T(8,128)(2,1)} %t_h.1, ...), custom_call_target="tpu_custom_call" | custom-call | tf_op jit(solution)/shard_map/pallas_call | solution.py:402
  24.5 1.5 %copy.11 = f32[2,4,8,256]{3,2,1,0:T(8,128)} copy(f32[2,4,8,256]{3,2,1,0:T(8,128)} %shard_map.91) | data formatting | bytes 131072

commit v3 on v2

--- a/solution.py
+++ b/solution.py
@@ -396,7 +396,8 @@
                 out_ref[r, 2 * w + v] = joined(last, 16 * v) + acc[i + v]
 
 
-def body(rs, order, basis, near, lcp, tr, bcp, bt, ccp):
+def body(*args):
+    rs, order, basis, _, lcp, tr, bcp, bt, ccp = args
     hbm = pl.BlockSpec(memory_space=pltpu.HBM)
     dma = pltpu.SemaphoreType.DMA
     return pl.pallas_call(
@@ -442,9 +443,9 @@
             dma((1,)),
         ],
         compiler_params=pltpu.CompilerParams(
-            collective_id=0, has_side_effects=True, vmem_limit_bytes=56 * 2**20
+            collective_id=0, has_side_effects=True, vmem_limit_bytes=40 * 2**20
         ),
-    )(rs, order, basis, near, lcp, tr, bcp, bt, ccp)
+    )(*(pltpu.with_memory_space_constraint(v, pltpu.HBM) for v in args))
 
 
 def solution(mesh):

time: 26.1 us -> 24.6 us (0.943)
  local copies, waits for them, and re-layouts: 1.47 us -> 0.63 us
  Pallas kernels: 24.5 us -> 23.8 us
    unnamed x1, local copies, waits for them, and re-layouts: 1.47 us -> 0.63 us
    pallas_call x1, Pallas kernels: 24.5 us -> 23.8 us  [body(): pl.pallas_call(kernel, out_shape=jax.ShapeDtypeStruct((2, 4, 8, 256), F32...]
where the time goes in v3:
time: 24.6 us; the launch traced here: 24.5 us
  Pallas kernels  23.8 us (97%)
  local copies, waits for them, and re-layouts  0.63 us (3%)
    pallas_call x1, Pallas kernels, body(): pl.pallas_call(kernel, out_shape=jax.ShapeDtypeStruct((2, 4, 8, 256), F32...  23.8 us
    unnamed x1, local copies, waits for them, and re-layouts  0.63 us

profile of v3, /device:TPU:8, one launch (start us, length us, event | category | flops | bytes accessed | tf_op | source)
XLA Modules:
  0.0 24.5 jit_solution(3925296946840690662)
XLA Ops:
  0.0 23.8 %shard_map.91 = f32[2,4,8,256]{3,2,1,0:T(8,128)S(1)} custom-call(bf16[2,4,8,256]{3,2,1,0:T(8,128)(2,1)} %rs_h.1, s32[2,4,256]{2,1,0:T(4,128)} %order_h.1, bf16[2,4,64,256]{3,2,1,0:T(8,128)(2,1)} %basis_h.1, bf16[2,4,256,2304]{3,2,1,0:T(8,128)(2,1)} %near_h.1, bf16[2,4,64,1728]{3,2,1,0:T(8,128)(2,1)} %lcp_h.1, bf16[2,4,64,64]{3,2,1,0:T(8,128)(2,1)} %t_h.1, ...), custom_call_target="tpu_custom_call" | custom-call | tf_op jit(solution)/shard_map/pallas_call | solution.py:403
  23.8 0.6 %copy.11 = f32[2,4,8,256]{3,2,1,0:T(8,128)} copy(f32[2,4,8,256]{3,2,1,0:T(8,128)S(1)} %shard_map.91) | data formatting | bytes 131072

commit v4 on v3

--- a/solution.py
+++ b/solution.py
@@ -254,7 +254,7 @@
             to_y = (y + 2 * i + odd) % 4
             to_x = (x + dx) % 4
             copy = pltpu.make_async_remote_copy(
-                row, coarse.at[pl.ds((y % 2) * 4, 4), x],
+                row, coarse.at[(y % 2) * 4 + x],
                 p2_send.at[4 * i + dx], p2_recv.at[0],
                 device_id=(8 * to_y + to_z, 2 * to_x + c), device_id_type=MESH,
             )
@@ -268,7 +268,7 @@
                 @pl.when(odd == 0)
                 def _():
                     pltpu.make_async_copy(
-                        row, coarse.at[pl.ds((y % 2) * 4, 4), x], p2_recv.at[0]
+                        row, coarse.at[(y % 2) * 4 + x], p2_recv.at[0]
                     ).start()
             else:
                 copy.start()
@@ -361,7 +361,7 @@
         apart = 8 * half_id + i - pair
         near_row = (apart >= -1) & (apart <= 1)
         for xs in range(4):
-            sources.append(jnp.where(near_cols[xs] & near_row, 0.0, coarse[i, xs]))
+            sources.append(jnp.where(near_cols[xs] & near_row, 0.0, coarse[i // 4 * 4 + xs, i % 4]))
     here = joined(dot_nt(split(jnp.concatenate(sources, 1)), ccp[0, 0]))
     half[...] = here
     swap = pltpu.make_async_remote_copy(

time: 24.6 us -> 24.6 us (level)
  no operation moved by 1% of the time
where the time goes in v4:
time: 24.6 us; the launch traced here: 24.5 us
  Pallas kernels  23.8 us (97%)
  local copies, waits for them, and re-layouts  0.63 us (3%)
    pallas_call x1, Pallas kernels, body(): pl.pallas_call(kernel, out_shape=jax.ShapeDtypeStruct((2, 4, 8, 256), F32...  23.8 us
    unnamed x1, local copies, waits for them, and re-layouts  0.63 us

profile of v4, /device:TPU:8, one launch (start us, length us, event | category | flops | bytes accessed | tf_op | source)
XLA Modules:
  0.0 24.5 jit_solution(6142409769640949211)
XLA Ops:
  0.0 23.8 %shard_map.91 = f32[2,4,8,256]{3,2,1,0:T(8,128)S(1)} custom-call(bf16[2,4,8,256]{3,2,1,0:T(8,128)(2,1)} %rs_h.1, s32[2,4,256]{2,1,0:T(4,128)} %order_h.1, bf16[2,4,64,256]{3,2,1,0:T(8,128)(2,1)} %basis_h.1, bf16[2,4,256,2304]{3,2,1,0:T(8,128)(2,1)} %near_h.1, bf16[2,4,64,1728]{3,2,1,0:T(8,128)(2,1)} %lcp_h.1, bf16[2,4,64,64]{3,2,1,0:T(8,128)(2,1)} %t_h.1, ...), custom_call_target="tpu_custom_call" | custom-call | tf_op jit(solution)/shard_map/pallas_call | solution.py:403
  23.8 0.6 %copy.11 = f32[2,4,8,256]{3,2,1,0:T(8,128)} copy(f32[2,4,8,256]{3,2,1,0:T(8,128)S(1)} %shard_map.91) | data formatting | bytes 131072

commit v5 on v4

--- a/solution.py
+++ b/solution.py
@@ -62,7 +62,7 @@
     out_ref,
     rs, order, basis, near, lcp, tr, bcp, bt, ccp,
     sel, tcat, ohalo, lwin, bwin, pack, row, coarse, half, other_half,
-    acc, basis_in,
+    acc, basis_in, through,
     load_sem, near_sem,
     p1_send, p1_recv, p2_send, p2_recv,
     o_send, o_recv, l_send, l_recv, b_send, b_recv, x_send, x_recv,
@@ -184,7 +184,7 @@
     for n, d in enumerate(far_first):
         t = (own + d) % 16
         send(
-            pack.at[own], pack.at[own], p1_send.at[n], p1_recv.at[0],
+            pack.at[own], pack.at[own], p1_send.at[n], p1_recv.at[z // 4],
             (8 * y + t // 2, 2 * x + t % 2),
         )
     mine, mid, cols = pl.ds(1, 2), pl.ds(2, 2), pl.ds(1, 4)
@@ -232,46 +232,62 @@
                 total = term if total is None else total + term
         return total
 
+    for r in range(2):
+        for w in range(2):
+            i = (2 * r + w) * 256
+            down_two = dot_nn(tr[r, 2 * w : 2 * w + 2].reshape(128, 64), bt[0, w])
+            down_high = down_two.astype(BF16)
+            through[i : i + 128] = down_high
+            through[i + 128 : i + 256] = (down_two - down_high.astype(F32)).astype(BF16)
     for i in range(8):
         near_loads[i].wait()
         acc[i] = near_terms(i, True)
         basis_in[i] = dot_nt(basis[i // 4, i % 4], sel[i]).astype(BF16)
 
-    arrived = pack.at[pl.ds(0, 15)]
-    pltpu.make_async_copy(arrived, arrived, p1_recv.at[0]).wait()
-    for zp in range(4):
-        pairs = [pack[4 * zp + k] + pack[4 * zp + 2 + k] for k in range(2)]
-        turned = [pltpu.roll(p, 64, 1) for p in pairs]
-        row[zp] = jnp.concatenate(
-            [jnp.where(low4, pairs[0], turned[1]), jnp.where(low4, turned[0], pairs[1])], 0
-        )
     my_half = y // 2
     odd = jnp.where(z % 2 == my_half, 0, 1)
     to_z = z + odd * (1 - 2 * (z % 2))
+    slot = (y % 2) * 4 + x
     stage2 = []
-    for i in range(2):
-        for dx in range(4):
-            to_y = (y + 2 * i + odd) % 4
-            to_x = (x + dx) % 4
-            copy = pltpu.make_async_remote_copy(
-                row, coarse.at[(y % 2) * 4 + x],
-                p2_send.at[4 * i + dx], p2_recv.at[0],
-                device_id=(8 * to_y + to_z, 2 * to_x + c), device_id_type=MESH,
+    for g in range(2):
+        for others in (7, 8):
+
+            @pl.when((z // 4 == g) == (others == 7))
+            def _():
+                arrived = pack.at[pl.ds(0, others)]
+                pltpu.make_async_copy(arrived, arrived, p1_recv.at[g]).wait()
+
+        for zp in (2 * g, 2 * g + 1):
+            pairs = [pack[4 * zp + k] + pack[4 * zp + 2 + k] for k in range(2)]
+            turned = [pltpu.roll(p, 64, 1) for p in pairs]
+            row[zp] = jnp.concatenate(
+                [jnp.where(low4, pairs[0], turned[1]), jnp.where(low4, turned[0], pairs[1])], 0
             )
-            stage2.append(copy)
-            if i == 0 and dx == 0:
-
-                @pl.when(odd == 1)
-                def _():
+        two = pl.ds(2 * g, 2)
+        for i in range(2):
+            for dx in (2, 1, 3, 0):
+                to_y = (y + 2 * i + odd) % 4
+                to_x = (x + dx) % 4
+                copy = pltpu.make_async_remote_copy(
+                    row.at[two], coarse.at[slot, two],
+                    p2_send.at[len(stage2)], p2_recv.at[g],
+                    device_id=(8 * to_y + to_z, 2 * to_x + c), device_id_type=MESH,
+                )
+                itself = i == 0 and dx == 0
+                stage2.append((itself, copy))
+                if itself:
+
+                    @pl.when(odd == 1)
+                    def _():
+                        copy.start()
+
+                    @pl.when(odd == 0)
+                    def _():
+                        pltpu.make_async_copy(
+                            row.at[two], coarse.at[slot, two], p2_recv.at[g]
+                        ).start()
+                else:
                     copy.start()
-
-                @pl.when(odd == 0)
-                def _():
-                    pltpu.make_async_copy(
-                        row, coarse.at[(y % 2) * 4 + x], p2_recv.at[0]
-                    ).start()
-            else:
-                copy.start()
 
     def arrive(ref, sem):
         pltpu.make_async_copy(ref, ref, sem).wait()
@@ -349,31 +365,46 @@
     out = dot_nt(jnp.concatenate(both, 0), bcp[0].reshape(128, 1728))
     box_far = jnp.where(low8, joined(out, 0), joined(out, 16))
 
+    for copy in sends:
+        copy.wait_send()
     loads[7].wait()
-    arrive(coarse, p2_recv.at[0])
     lane = lax.broadcasted_iota(jnp.int32, (8, 128), 1)
     near_cols = []
     for xs in range(4):
         apart = 2 * xs + lane // 64 - gy
         near_cols.append((apart >= -1) & (apart <= 1))
-    sources = []
-    for i in range(8):
-        apart = 8 * half_id + i - pair
-        near_row = (apart >= -1) & (apart <= 1)
-        for xs in range(4):
-            sources.append(jnp.where(near_cols[xs] & near_row, 0.0, coarse[i // 4 * 4 + xs, i % 4]))
-    here = joined(dot_nt(split(jnp.concatenate(sources, 1)), ccp[0, 0]))
+    here = None
+    for g in range(2):
+        arrive(coarse.at[pl.ds(0, 4)], p2_recv.at[g])
+        for yb in range(2):
+            sources = []
+            for zp in (2 * g, 2 * g + 1):
+                apart = 8 * half_id + 4 * yb + zp - pair
+                near_row = (apart >= -1) & (apart <= 1)
+                for xs in range(4):
+                    sources.append(
+                        jnp.where(near_cols[xs] & near_row, 0.0, coarse[4 * yb + xs, zp])
+                    )
+            first = (4 * yb + 2 * g) * 512
+            term = dot_nt(
+                split(jnp.concatenate(sources, 1)), ccp[0, 0, :, first : first + 1024]
+            )
+            here = term if here is None else here + term
+    here = joined(here)
     half[...] = here
     swap = pltpu.make_async_remote_copy(
         half, other_half, x_send.at[0], x_recv.at[0], device_id=(partner, gy), device_id_type=MESH
     )
     swap.start()
+    both = [split(jnp.where(low8, box_far, 0.0)), split(jnp.where(low8, 0.0, box_far))]
+    out = dot_nt(jnp.concatenate(both, 0), tcat[...])
+    for r in range(2):
+        for w in range(2):
+            leaf_far[r, w] += joined(out[:, 128 * r : 128 * r + 128], 16 * w)
     for i in range(8):
         acc[i] = joined(dot_nt(split(acc[i]), sel[i]))
-    for copy in sends:
-        copy.wait_send()
-    for n, copy in enumerate(stage2):
-        if n == 0:
+    for itself, copy in stage2:
+        if itself:
 
             @pl.when(odd == 1)
             def _():
@@ -383,12 +414,11 @@
     swap.wait()
 
     coarse_far = here + other_half[...]
-    box_down = joined(dot_nt(split(coarse_far), bt_all)) + box_far
-    both = [split(jnp.where(low8, box_down, 0.0)), split(jnp.where(low8, 0.0, box_down))]
-    out = dot_nt(jnp.concatenate(both, 0), tcat[...])
+    out = joined(dot_nt(split(coarse_far), through[...]))
     for r in range(2):
         for w in range(2):
-            leaf_down = joined(out[:, 128 * r : 128 * r + 128], 16 * w) + leaf_far[r, w]
+            i = (2 * r + w) * 256
+            leaf_down = out[:, i : i + 128] + out[:, i + 128 : i + 256] + leaf_far[r, w]
             both = [split(jnp.where(low8, leaf_down, 0.0)), split(jnp.where(low8, 0.0, leaf_down))]
             i = 4 * r + 2 * w
             last = dot_nn(jnp.concatenate(both, 0), basis_in[i : i + 2].reshape(128, 256))
@@ -427,12 +457,13 @@
             pltpu.VMEM((8, 64), F32),
             pltpu.VMEM((8, 8, 256), F32),
             pltpu.VMEM((8, 64, 256), BF16),
+            pltpu.VMEM((1024, 64), BF16),
             dma((8,)),
             dma((8,)),
             dma((15,)),
-            dma((1,)),
-            dma((8,)),
-            dma((1,)),
+            dma((2,)),
+            dma((16,)),
+            dma((2,)),
             dma((8,)),
             dma((4,)),
             dma((8,)),

time: 24.6 us -> 24.1 us (0.980)
  Pallas kernels: 23.8 us -> 23.2 us
    pallas_call x1, Pallas kernels: 23.8 us -> 23.2 us  [body(): pl.pallas_call(kernel, out_shape=jax.ShapeDtypeStruct((2, 4, 8, 256), F32...]
where the time goes in v5:
time: 24.1 us; the launch traced here: 23.8 us
  Pallas kernels  23.2 us (96%)
  local copies, waits for them, and re-layouts  0.63 us (3%)
    pallas_call x1, Pallas kernels, body(): pl.pallas_call(kernel, out_shape=jax.ShapeDtypeStruct((2, 4, 8, 256), F32...  23.2 us
    unnamed x1, local copies, waits for them, and re-layouts  0.63 us

profile of v5, /device:TPU:8, one launch (start us, length us, event | category | flops | bytes accessed | tf_op | source)
XLA Modules:
  0.0 23.8 jit_solution(2068147881934754008)
XLA Ops:
  0.0 23.2 %shard_map.91 = f32[2,4,8,256]{3,2,1,0:T(8,128)S(1)} custom-call(bf16[2,4,8,256]{3,2,1,0:T(8,128)(2,1)} %rs_h.1, s32[2,4,256]{2,1,0:T(4,128)} %order_h.1, bf16[2,4,64,256]{3,2,1,0:T(8,128)(2,1)} %basis_h.1, bf16[2,4,256,2304]{3,2,1,0:T(8,128)(2,1)} %near_h.1, bf16[2,4,64,1728]{3,2,1,0:T(8,128)(2,1)} %lcp_h.1, bf16[2,4,64,64]{3,2,1,0:T(8,128)(2,1)} %t_h.1, ...), custom_call_target="tpu_custom_call" | custom-call | tf_op jit(solution)/shard_map/pallas_call | solution.py:433
  23.2 0.6 %copy.11 = f32[2,4,8,256]{3,2,1,0:T(8,128)} copy(f32[2,4,8,256]{3,2,1,0:T(8,128)S(1)} %shard_map.91) | data formatting | bytes 131072
